TPU v7x, 256 devices: a whole 4x4x8 slice. The times are simulated.
256 devices in a mesh: seq: 32 (over x, y, core), head: 8 (over z).
Axes of the slice: x: 4, y: 4, z: 8, core: 2. Of those that a mesh axis runs over, the one named last changes fastest.
Arguments:
- positions: int32 [16384], P('seq'), may hold values from 65535 to 98301, as said below
- queries: bfloat16 [16384, 32, 128], P('seq', 'head'), may hold values from -16 to 16
- keys: bfloat16 [16384, 16, 128], P('seq', 'head'), may hold values from -16 to 16
- values: bfloat16 [16384, 16, 128], P('seq', 'head'), may hold values from -6 to 6
- out_weight: bfloat16 [4096, 5376], P('head', 'seq'), may hold values from -0.1875 to 0.1875
- post_gain: float32 [5376], P('head'), may hold values from 0.25 to 1.75
- residual: bfloat16 [16384, 5376], P('seq', 'head'), may hold values from -6 to 6
Outputs:
- layer_out: bfloat16 [16384, 5376], P('seq', 'head')
Inputs may be any that keep to these rules, and one draw needn't show every extreme that they name: `positions`: strictly rising, by 1 or 2 from one token to the next; the last token's position is the most.
All inputs are finite; a program needn't handle non-finite values.
Results may differ from a plain program's by a relative error of at most 0.015.
Values may be sent and summed in bfloat16 or wider, within the bound.
No kernel may reach another device: no remote copies, remote signals or barrier semaphores. Data moves between devices by JAX's collectives and lax.ppermute only.
A program may use at most 64 MiB of HBM per device.

v0:
```python
import jax
import jax.numpy as jnp
from jax import lax
from jax.sharding import PartitionSpec as P

D = 5376
QUERY_HEADS = 32
KEY_VALUE_HEADS = 16
VISIBLE_SPAN = 1024
EPS = 1e-06
SCALE = 168.0 ** (-0.5)


def passed_along(value, axis, steps):
    count = lax.axis_size(axis)
    initial, last = (max(0, -steps), min(count, count - steps))
    return lax.ppermute(value, axis, [(source, source + steps) for source in range(initial, last)])


def copy_for_each(array, axis):
    length = lax.axis_size(axis)
    return lax.all_to_all(
        jnp.broadcast_to(array[None], (length, *array.shape)), axis, 0, 0, tiled=True
    )


def of_everyone(array, axis):
    return copy_for_each(array, axis).sum(axis=0)


def rotate(x, positions):
    half = x.shape[-1] // 2
    inverse = 10000.0 ** (-2.0 * jnp.arange(half, dtype=jnp.float32) / x.shape[-1])
    angle = positions.astype(jnp.float32)[:, None] * inverse[None, :]
    cosine = jnp.concatenate([jnp.cos(angle), jnp.cos(angle)], -1)[:, None, :]
    sine = jnp.concatenate([jnp.sin(angle), jnp.sin(angle)], -1)[:, None, :]
    source = x.astype(jnp.float32)
    turned = jnp.concatenate([-source[..., half:], source[..., :half]], -1)
    return (source * cosine + turned * sine).astype(jnp.bfloat16)


def on_device(positions, queries, keys, values, out_weight, post_gain, residual):
    rows = queries.shape[0]
    kv_heads = keys.shape[1]
    query_groups = QUERY_HEADS // KEY_VALUE_HEADS
    q_rot = rotate(queries, positions)
    stacked = jnp.stack([rotate(keys, positions), values], 0)
    reach = (VISIBLE_SPAN + rows - 2) // rows
    pieces = []
    carried = stacked
    for hop in range(reach):
        carried = passed_along(carried, "seq", 1)
        pieces.insert(0, carried)
    extended = jnp.concatenate(pieces + [stacked], axis=1)
    extra = extended.shape[1] - rows
    anchor = lax.axis_index("seq") * rows
    block_length = min(512, rows)
    query_tile_rows = q_rot.reshape(block_length, kv_heads, query_groups, -1)
    key_block = extended[0, 0 : extra + block_length]
    value_block = extended[1, 0 : extra + block_length]
    scores = (
        jnp.einsum("qhgd,khd->hgqk", query_tile_rows, key_block, preferred_element_type=jnp.float32)
        * SCALE
    )
    query_index = anchor + 0 + jnp.arange(block_length, dtype=jnp.int32)
    key_index = anchor - extra + 0 + jnp.arange(extra + block_length, dtype=jnp.int32)
    gap = query_index[:, None] - key_index[None, :]
    allowed = (gap >= 0) & (gap < VISIBLE_SPAN) & (key_index[None, :] >= 0)
    scores = jnp.where(allowed, scores, -1e30)
    top = jnp.max(scores, axis=-1, keepdims=True)
    weights = jnp.exp(scores - top)
    probs = (weights / jnp.sum(weights, axis=-1, keepdims=True)).astype(jnp.bfloat16)
    context = jnp.einsum("hgqk,khd->qhgd", probs, value_block, preferred_element_type=jnp.float32)
    outputs = context.astype(jnp.bfloat16).reshape(block_length, -1)
    context = outputs
    partial_value = jnp.dot(
        context,
        lax.all_gather(out_weight, "seq", axis=1, tiled=True),
        preferred_element_type=jnp.float32,
    )
    attended = lax.psum_scatter(
        partial_value.astype(jnp.bfloat16), "head", scatter_dimension=1, tiled=True
    ).astype(jnp.float32)
    squares = of_everyone(jnp.sum(attended * attended, axis=1), "head")
    scaled = attended * lax.rsqrt(squares / D + EPS)[:, None]
    result = residual.astype(jnp.float32) + post_gain[None, :] * scaled
    return result.astype(jnp.bfloat16)


def solution(mesh):
    return jax.shard_map(
        on_device,
        mesh=mesh,
        in_specs=(
            P("seq"),
            P("seq", "head", None),
            P("seq", "head", None),
            P("seq", "head", None),
            P("head", "seq"),
            P("head"),
            P("seq", "head"),
        ),
        out_specs=P("seq", "head"),
        check_vma=False,
    )
```

profile of v0, /device:TPU:2, one launch (start us, length us, event | category | flops | bytes accessed | tf_op | source)
XLA Modules:
  0.0 164.7 jit_solution(17591090239701363710)
XLA Ops:
  6.5 0.0 copy-start.3
  6.5 0.0 all-gather.2.cloned.1.call-start
  6.5 0.7 all-gather.2.cloned.1.call-update
  7.3 0.0 reduce-scatter.2.cloned.1.call-start
  7.3 0.7 convert_element_type.39
  8.0 1.0 copy.44
  9.0 1.0 multiply_cosine_fusion
  10.0 0.2 pad_maximum_fusion.1
  10.2 0.0 copy-start
  10.2 1.0 copy_convert_fusion
  11.3 0.2 slice_negate_fusion.1
  11.5 0.0 copy-done.3
  11.5 0.2 fusion.24
  11.7 0.0 copy-start.1
  11.7 0.9 pad_maximum_fusion
  12.6 1.9 %collective-permute-start = (bf16[2,512,2,128]{3,1,2,0:T(8,128)(2,1)}, bf16[2,512,2,128]{3,1,2,0:T(8,128)(2,1)}, u32[]{:S(2)}, u32[]{:S(2)}) collective-permute-start(bf16[2,512,2,128]{3,1,2,0:T(8,128)(2,1)} %pad_maximum_fusion), channel_id=1, source_target_pairs={{0,8},{8,16},{16,24},{24,32},{32,40},{40,48},{48,56},{56,64},{64,7... | collective-permute-start | bytes 1572872 | tf_op jit(solution)/shard_map/ppermute | solution.py:17
  14.5 0.0 copy-done.1
  14.5 0.0 copy-done
  14.5 0.1 convert_element_type.41
  14.6 0.1 slice.29
  14.8 0.0 copy-start.2
  14.8 0.6 slice_negate_fusion
  15.4 1.6 fusion.16
  17.1 0.0 copy-start.5
  17.1 8.4 %collective-permute-done = bf16[2,512,2,128]{3,1,2,0:T(8,128)(2,1)} collective-permute-done((bf16[2,512,2,128]{3,1,2,0:T(8,128)(2,1)}, bf16[2,512,2,128]{3,1,2,0:T(8,128)(2,1)}, u32[]{:S(2)}, u32[]{:S(2)}) %collective-permute-start) | collective-permute-done | bytes 524320 | tf_op jit(solution)/shard_map/ppermute | solution.py:17
  25.5 1.9 %collective-permute-start.1 = (bf16[2,512,2,128]{3,1,2,0:T(8,128)(2,1)}, bf16[2,512,2,128]{3,1,2,0:T(8,128)(2,1)S(1)}, u32[]{:S(2)}, u32[]{:S(2)}) collective-permute-start(bf16[2,512,2,128]{3,1,2,0:T(8,128)(2,1)} %collective-permute-done), channel_id=1, source_target_pairs={{0,8},{8,16},{16,24},{24,32},{32,40},{40,48},{48,56},{56,64},{64,7... | collective-permute-start | bytes 1572872 | tf_op jit(solution)/shard_map/ppermute | solution.py:17
  27.4 1.2 fusion.7
  28.6 11.5 %collective-permute-done.1 = bf16[2,512,2,128]{3,1,2,0:T(8,128)(2,1)S(1)} collective-permute-done((bf16[2,512,2,128]{3,1,2,0:T(8,128)(2,1)}, bf16[2,512,2,128]{3,1,2,0:T(8,128)(2,1)S(1)}, u32[]{:S(2)}, u32[]{:S(2)}) %collective-permute-start.1) | collective-permute-done | bytes 524320 | tf_op jit(solution)/shard_map/ppermute | solution.py:17
  40.1 0.0 copy-done.2
  40.1 1.2 maximum_maximum_fusion
  41.3 0.0 copy-done.5
  41.3 7.4 %fusion.27 = (f32[2,2,512]{2,1,0:T(2,128)S(1)}, f32[2,2,512,1536]{2,3,1,0:T(8,128)}) fusion(pred[512,1536]{0,1:T(8,128)(4,1)S(1)} %fusion.7, bf16[2,1536,2,128]{3,1,2,0:T(8,128)(2,1)S(1)} %maximum_maximum_fusion, bf16[512,2,2,128]{3,2,1,0:T(2,128)(2,1)S(1)} %bitcast.46), kind=kOutput, calls=%fused_computation.51 | convolution fusion | flops 817890816 | bytes 14688256 | tf_op jit(solution)/shard_map/sub | solution.py:71
  48.8 6.1 %fusion.14 = bf16[2,128,2,512]{3,1,2,0:T(8,128)(2,1)S(1)} fusion(f32[2,2,512,1536]{2,3,1,0:T(8,128)} %get-tuple-element.10, f32[2,2,512]{2,1,0:T(2,128)S(1)} %get-tuple-element.9, bf16[2,1536,2,128]{3,1,2,0:T(8,128)(2,1)S(1)} %maximum_maximum_fusion), kind=kOutput, calls=%fused_computation.22 | convolution fusion | flops 811859968 | bytes 13901824 | tf_op jit(solution)/shard_map/hgqk,khd->qhgd/dot_general | solution.py:73
  54.9 12.6 %all-gather.2.cloned.1.call-done = bf16[512,5376]{0,1:T(8,128)(2,1)} async-done(((bf16[512,168]{0,1:T(8,128)(2,1)}), bf16[512,5376]{0,1:T(8,128)(2,1)}) %all-gather.2.cloned.1.call-update) | async-done | bytes 5505040 | tf_op jit(solution)/shard_map/all_gather | solution.py:78
  67.4 7.3 %convolution_convert_fusion = bf16[512,5376]{0,1:T(8,128)(2,1)} fusion(bf16[512,5376]{0,1:T(8,128)(2,1)} %all-gather.2.cloned.1.call-done, bf16[512,512]{0,1:T(8,128)(2,1)S(1)} %bitcast.47), kind=kOutput, calls=%fused_computation.5 | convolution fusion | flops 2821324800 | bytes 11534336 | tf_op jit(solution)/shard_map/dot_general | solution.py:76
  74.7 0.0 copy-start.4
  74.7 0.0 copy-start.6
  74.7 0.0 reduce-scatter.2.cloned.1.call-update
  74.8 67.6 %reduce-scatter.2.cloned.1.call-done = bf16[512,672]{0,1:T(8,128)(2,1)} async-done(((bf16[512,5376]{0,1:T(8,128)(2,1)}), bf16[512,672]{0,1:T(8,128)(2,1)}) %reduce-scatter.2.cloned.1.call-update) | async-done | bytes 688144 | tf_op jit(solution)/shard_map/reduce_scatter | solution.py:81
  142.4 1.3 fusion.8
  143.7 11.9 %all_to_all.6 = f32[8,1,512]{2,1,0:T(1,128)S(1)} all-to-all(f32[8,1,512]{2,1,0:T(1,128)S(1)} %broadcast_in_dim.10), channel_id=1, replica_groups=mesh['seq'=32,'head'=8] {'head'}, dimensions={0} | all-to-all | bytes 32768 | tf_op jit(solution)/shard_map/all_to_all | solution.py:22
  155.6 0.0 copy-done.4
  155.7 0.0 copy-done.6
  155.7 2.2 %fusion.11 = bf16[512,672]{0,1:T(8,128)(2,1)} fusion(bf16[512,672]{0,1:T(8,128)(2,1)} %reduce-scatter.2.cloned.1.call-done, bf16[512,672]{0,1:T(8,128)(2,1)S(1)} %copy-done.4, f32[512]{0:T(512)S(1)} %add_rsqrt_fusion, f32[672]{0:T(1024)S(1)} %copy-done.6), kind=kLoop, calls=%fused_computation.20 | loop fusion | flops 2064384 | bytes 2069120 | tf_op jit(solution)/shard_map/convert_element_type | solution.py:87
  (7 shorter events, 0.1 us)
Async XLA Ops:
  6.5 4.9 %copy-start.3 = (bf16[512,2,128]{2,1,0:T(2,128)(2,1)S(1)}, bf16[512,2,128]{2,1,0:T(2,128)(2,1)}, u32[]{:S(2)}) copy-start(bf16[512,2,128]{2,1,0:T(2,128)(2,1)} %param.9) | copy-start | bytes 786436
  6.5 60.9 %all-gather.2.cloned.1.call-start = ((), (), s32[]{:S(2)}) async-start(), calls=%async_computation.2 | async-start | bytes 5677056 | tf_op jit(solution)/shard_map/all_gather | solution.py:78
  7.3 135.1 %reduce-scatter.2.cloned.1.call-start = ((), (), s32[]{:S(2)}) async-start(), calls=%async_computation.3 | async-start | bytes 6193152 | tf_op jit(solution)/shard_map/reduce_scatter | solution.py:81
  10.2 4.3 %copy-start = (bf16[512,4,128]{2,1,0:T(4,128)(2,1)S(1)}, bf16[512,4,128]{2,1,0:T(4,128)(2,1)}, u32[]{:S(2)}) copy-start(bf16[512,4,128]{2,1,0:T(4,128)(2,1)} %param.8) | copy-start | bytes 1572868
  11.7 2.8 %copy-start.1 = (bf16[1,512,2,128]{3,1,2,0:T(8,128)(2,1)}, bf16[1,512,2,128]{3,1,2,0:T(8,128)(2,1)S(1)}, u32[]{:S(2)}) copy-start(bf16[1,512,2,128]{3,1,2,0:T(8,128)(2,1)S(1)} %fusion.24) | copy-start | bytes 786436
  12.6 12.9 %collective-permute-start = (bf16[2,512,2,128]{3,1,2,0:T(8,128)(2,1)}, bf16[2,512,2,128]{3,1,2,0:T(8,128)(2,1)}, u32[]{:S(2)}, u32[]{:S(2)}) collective-permute-start(bf16[2,512,2,128]{3,1,2,0:T(8,128)(2,1)} %pad_maximum_fusion), channel_id=1, source_target_pairs={{0,8},{8,16},{16,24},{24,32},{32,40},{40,48},{48,56},{56,64},{64,7... | collective-permute-start | bytes 1572872 | tf_op jit(solution)/shard_map/ppermute | solution.py:17
  14.8 25.3 %copy-start.2 = (bf16[1,512,2,128]{3,1,2,0:T(8,128)(2,1)S(1)}, bf16[1,512,2,128]{3,1,2,0:T(8,128)(2,1)}, u32[]{:S(2)}) copy-start(bf16[1,512,2,128]{3,1,2,0:T(8,128)(2,1)} %copy-done.1) | copy-start | bytes 786436
  17.1 24.3 %copy-start.5 = (bf16[512,4,128]{2,1,0:T(4,128)(2,1)S(1)}, bf16[512,4,128]{2,1,0:T(4,128)(2,1)}, u32[]{:S(2)}) copy-start(bf16[512,4,128]{2,1,0:T(4,128)(2,1)} %fusion.16) | copy-start | bytes 1572868
  25.5 14.7 %collective-permute-start.1 = (bf16[2,512,2,128]{3,1,2,0:T(8,128)(2,1)}, bf16[2,512,2,128]{3,1,2,0:T(8,128)(2,1)S(1)}, u32[]{:S(2)}, u32[]{:S(2)}) collective-permute-start(bf16[2,512,2,128]{3,1,2,0:T(8,128)(2,1)} %collective-permute-done), channel_id=1, source_target_pairs={{0,8},{8,16},{16,24},{24,32},{32,40},{40,48},{48,56},{56,64},{64,7... | collective-permute-start | bytes 1572872 | tf_op jit(solution)/shard_map/ppermute | solution.py:17
  74.7 80.9 %copy-start.4 = (bf16[512,672]{0,1:T(8,128)(2,1)S(1)}, bf16[512,672]{0,1:T(8,128)(2,1)}, u32[]{:S(2)}) copy-start(bf16[512,672]{0,1:T(8,128)(2,1)} %param.13) | copy-start | bytes 2064388
  74.7 80.9 %copy-start.6 = (f32[672]{0:T(1024)S(1)}, f32[672]{0:T(1024)}, u32[]{:S(2)}) copy-start(f32[672]{0:T(1024)} %param.12) | copy-start | bytes 8068
Sparse Core Ops, SparseCore 0:
  9.9 57.4 all-gather.1
  74.9 67.4 reduce-scatter.1
where the time goes:
time: 165 us
  waiting for transfers between devices  101 us (61%)
  matrix products  20.9 us (13%)
  between operations  13.6 us (8%)
  other arithmetic  12.5 us (8%)
  blocking collectives  11.9 us (7%)
  starting transfers between devices  3.86 us (2%)
    reduce_scatter x1, waiting for transfers between devices, on_device(): lax.psum_scatter(partial_value.astype(jnp.bfloat16), 'head', scatter_dime...  67.6 us
    ppermute x2, waiting for transfers between devices, passed_along(): lax.ppermute(value, axis, [(source, source + steps) for source in range(i...  19.9 us
    all_gather x1, waiting for transfers between devices, on_device(): lax.all_gather(out_weight, 'seq', axis=1, tiled=True)  12.6 us
    all_to_all x1, blocking collectives, copy_for_each(): lax.all_to_all(jnp.broadcast_to(array[None], (length, *array.shape)), axi...  11.9 us
    sub x1, matrix products, on_device(): weights = jnp.exp(scores - top)  7.44 us
    dot_general x1, matrix products, on_device(): jnp.dot(context, lax.all_gather(out_weight, 'seq', axis=1, tiled=True), p...  7.32 us
    dot_general x1, matrix products, on_device(): jnp.einsum('hgqk,khd->qhgd', probs, value_block, preferred_element_type=j...  6.11 us
    ppermute x2, starting transfers between devices, passed_along(): lax.ppermute(value, axis, [(source, source + steps) for source in range(i...  3.82 us
  transfers between devices with their start and end apart: 4, of which 4 were waited for; matrix products, arithmetic and copies ran while one was open for 14% of the time, Pallas kernels for 0%

commit v1 on v0

--- a/solution.py
+++ b/solution.py
@@ -9,6 +9,11 @@
 VISIBLE_SPAN = 1024
 EPS = 1e-06
 SCALE = 168.0 ** (-0.5)
+
+
+def swapped_in(x, name, dim):
+    sent = jnp.stack([x] * lax.axis_size(name))
+    return jnp.concatenate(lax.all_to_all(sent, name, 0, 0), axis=dim)
 
 
 def passed_along(value, axis, steps):
@@ -74,9 +79,7 @@
     outputs = context.astype(jnp.bfloat16).reshape(block_length, -1)
     context = outputs
     partial_value = jnp.dot(
-        context,
-        lax.all_gather(out_weight, "seq", axis=1, tiled=True),
-        preferred_element_type=jnp.float32,
+        context, swapped_in(out_weight, "seq", 1), preferred_element_type=jnp.float32
     )
     attended = lax.psum_scatter(
         partial_value.astype(jnp.bfloat16), "head", scatter_dimension=1, tiled=True

time: 165 us -> 216 us (1.31)
  waiting for transfers between devices: 101 us -> 143 us
  starting transfers between devices: 3.86 us -> 11.8 us
  local copies, waits for them, and re-layouts: 1.14 us -> 3.87 us
    ppermute x2, waiting for transfers between devices: 19.9 us -> 75.3 us  [passed_along(): lax.ppermute(value, axis, [(source, source + steps) for source in range(i...]
    all_gather x1 -> x0, waiting for transfers between devices: 12.6 us -> none  [on_device(): lax.all_gather(out_weight, 'seq', axis=1, tiled=True)]
    all_to_all x0 -> x1, starting transfers between devices: none -> 7.8 us  [swapped_in(): return jnp.concatenate(lax.all_to_all(sent, name, 0, 0), axis=dim)]
    another operation x0 -> x1, local copies, waits for them, and re-layouts: none -> 3.67 us  [swapped_in(): sent = jnp.stack([x] * lax.axis_size(name))]
  transfers between devices with their start and end apart: 4 -> 4, of which waited for: 4 -> 3; matrix products, arithmetic and copies ran while one was open for 14% -> 10% of each run, Pallas kernels for 0% -> 0%
where the time goes in v1:
time: 216 us; the launch traced here: 215 us
  waiting for transfers between devices  143 us (66%)
  matrix products  20.4 us (9%)
  between operations  13.6 us (6%)
  blocking collectives  11.9 us (6%)
  starting transfers between devices  11.8 us (5%)
  other arithmetic  10.8 us (5%)
  local copies, waits for them, and re-layouts  3.87 us (2%)
    ppermute x2, waiting for transfers between devices, passed_along(): lax.ppermute(value, axis, [(source, source + steps) for source in range(i...  75.3 us
    reduce_scatter x1, waiting for transfers between devices, on_device(): lax.psum_scatter(partial_value.astype(jnp.bfloat16), 'head', scatter_dime...  67.4 us
    all_to_all x1, blocking collectives, copy_for_each(): lax.all_to_all(jnp.broadcast_to(array[None], (length, *array.shape)), axi...  11.9 us
    all_to_all x1, starting transfers between devices, swapped_in(): return jnp.concatenate(lax.all_to_all(sent, name, 0, 0), axis=dim)  7.8 us
    sub x1, matrix products, on_device(): weights = jnp.exp(scores - top)  7.45 us
    dot_general x1, matrix products, on_device(): jnp.dot(context, swapped_in(out_weight, 'seq', 1), preferred_element_type...  7.34 us
    dot_general x1, matrix products, on_device(): jnp.einsum('hgqk,khd->qhgd', probs, value_block, preferred_element_type=j...  5.66 us
  transfers between devices with their start and end apart: 4, of which 3 were waited for; matrix products, arithmetic and copies ran while one was open for 10% of the time, Pallas kernels for 0%

profile of v1, /device:TPU:2, one launch (start us, length us, event | category | flops | bytes accessed | tf_op | source)
XLA Modules:
  0.0 215.2 jit_solution(13146769772019910893)
XLA Ops:
  6.5 3.7 %stack.11 = bf16[32,512,168]{1,2,0:T(8,128)(2,1)} broadcast(bf16[512,168]{0,1:T(8,128)(2,1)} %param.11), dimensions={1,2} | broadcast | bytes 5677056 | tf_op jit(solution)/shard_map/stack | solution.py:15
  10.2 0.0 copy-start.8
  10.2 0.0 copy-start.6
  10.2 0.0 copy-start.3
  10.2 7.8 %all-to-all-start = ((bf16[32,512,168]{1,2,0:T(8,128)(2,1)}), bf16[32,512,168]{1,2,0:T(8,128)(2,1)}, u32[]{:S(2)}, u32[]{:S(2)}) async-start(bf16[32,512,168]{1,2,0:T(8,128)(2,1)} %stack.11), calls=%async_computation | async-start | bytes 11010048 | tf_op jit(solution)/shard_map/all_to_all | solution.py:16
  18.0 0.0 reduce-scatter.2.cloned.1.call-start
  18.1 0.0 copy-done.8
  18.1 1.0 multiply_cosine_fusion
  19.1 0.0 copy-done.6
  19.1 0.2 pad_maximum_fusion.1
  19.4 0.0 copy-done.3
  19.4 0.0 copy-start
  19.4 0.2 slice_negate_fusion.1
  19.6 0.2 fusion.24
  19.9 0.0 copy-start.1
  19.9 0.9 pad_maximum_fusion
  20.7 2.0 collective-permute-start
  22.8 0.0 copy-done.1
  22.8 0.0 copy-done
  22.8 0.1 convert_element_type.41
  22.9 0.1 slice.29
  23.1 0.0 copy-start.2
  23.1 0.6 slice_negate_fusion
  23.7 1.6 fusion.16
  25.3 0.0 copy-start.5
  25.3 65.7 %collective-permute-done = bf16[2,512,2,128]{3,1,2,0:T(8,128)(2,1)} collective-permute-done((bf16[2,512,2,128]{3,1,2,0:T(8,128)(2,1)}, bf16[2,512,2,128]{3,1,2,0:T(8,128)(2,1)}, u32[]{:S(2)}, u32[]{:S(2)}) %collective-permute-start) | collective-permute-done | bytes 524320 | tf_op jit(solution)/shard_map/ppermute | solution.py:22
  91.0 1.9 collective-permute-start.1
  92.9 1.2 fusion.7
  94.2 9.7 %collective-permute-done.1 = bf16[2,512,2,128]{3,1,2,0:T(8,128)(2,1)S(1)} collective-permute-done((bf16[2,512,2,128]{3,1,2,0:T(8,128)(2,1)}, bf16[2,512,2,128]{3,1,2,0:T(8,128)(2,1)S(1)}, u32[]{:S(2)}, u32[]{:S(2)}) %collective-permute-start.1) | collective-permute-done | bytes 524320 | tf_op jit(solution)/shard_map/ppermute | solution.py:22
  103.8 0.0 copy-done.2
  103.8 1.2 maximum_maximum_fusion
  105.0 0.0 copy-done.5
  105.0 7.4 %fusion.27 = (f32[2,2,512]{2,1,0:T(2,128)S(1)}, f32[2,2,512,1536]{2,3,1,0:T(8,128)}) fusion(pred[512,1536]{0,1:T(8,128)(4,1)S(1)} %fusion.7, bf16[2,1536,2,128]{3,1,2,0:T(8,128)(2,1)S(1)} %maximum_maximum_fusion, bf16[512,2,2,128]{3,2,1,0:T(2,128)(2,1)S(1)} %bitcast.49), kind=kOutput, calls=%fused_computation.51 | convolution fusion | flops 817890816 | bytes 14688256 | tf_op jit(solution)/shard_map/sub | solution.py:76
  112.4 5.7 %fusion.14 = bf16[2,128,2,512]{3,1,2,0:T(8,128)(2,1)S(1)} fusion(f32[2,2,512,1536]{2,3,1,0:T(8,128)} %get-tuple-element.10, f32[2,2,512]{2,1,0:T(2,128)S(1)} %get-tuple-element.9, bf16[2,1536,2,128]{3,1,2,0:T(8,128)(2,1)S(1)} %maximum_maximum_fusion), kind=kOutput, calls=%fused_computation.22 | convolution fusion | flops 811859968 | bytes 13901824 | tf_op jit(solution)/shard_map/hgqk,khd->qhgd/dot_general | solution.py:78
  118.1 0.0 all-to-all-done
  118.1 7.3 %convolution_convert_fusion = bf16[512,5376]{0,1:T(8,128)(2,1)} fusion(bf16[512,5376]{0,1:T(8,128)(2,1)} %bitcast.12, bf16[512,512]{0,1:T(8,128)(2,1)S(1)} %bitcast.50), kind=kOutput, calls=%fused_computation.5 | convolution fusion | flops 2821324800 | bytes 11534336 | tf_op jit(solution)/shard_map/dot_general | solution.py:81
  125.5 0.0 copy-start.4
  125.5 0.0 copy-start.7
  125.5 0.0 reduce-scatter.2.cloned.1.call-update
  125.5 67.4 %reduce-scatter.2.cloned.1.call-done = bf16[512,672]{0,1:T(8,128)(2,1)} async-done(((bf16[512,5376]{0,1:T(8,128)(2,1)}), bf16[512,672]{0,1:T(8,128)(2,1)}) %reduce-scatter.2.cloned.1.call-update) | async-done | bytes 688144 | tf_op jit(solution)/shard_map/reduce_scatter | solution.py:84
  192.9 1.3 fusion.8
  194.2 11.9 %all_to_all.11 = f32[8,1,512]{2,1,0:T(1,128)S(1)} all-to-all(f32[8,1,512]{2,1,0:T(1,128)S(1)} %broadcast_in_dim.10), channel_id=1, replica_groups=mesh['seq'=32,'head'=8] {'head'}, dimensions={0} | all-to-all | bytes 32768 | tf_op jit(solution)/shard_map/all_to_all | solution.py:27
  206.2 0.0 copy-done.4
  206.2 0.0 copy-done.7
  206.2 2.2 %fusion.11 = bf16[512,672]{0,1:T(8,128)(2,1)} fusion(bf16[512,672]{0,1:T(8,128)(2,1)} %reduce-scatter.2.cloned.1.call-done, bf16[512,672]{0,1:T(8,128)(2,1)S(1)} %copy-done.4, f32[512]{0:T(512)S(1)} %add_rsqrt_fusion, f32[672]{0:T(1024)S(1)} %copy-done.7), kind=kLoop, calls=%fused_computation.20 | loop fusion | flops 2064384 | bytes 2069120 | tf_op jit(solution)/shard_map/convert_element_type | solution.py:90
  (10 shorter events, 0.2 us)
Async XLA Ops:
  10.2 7.9 %copy-start.8 = (s32[512]{0:T(512)S(1)}, s32[512]{0:T(512)}, u32[]{:S(2)}) copy-start(s32[512]{0:T(512)} %param.7) | copy-start | bytes 6148
  10.2 8.9 %copy-start.6 = (bf16[512,2,128]{2,1,0:T(2,128)(2,1)S(1)}, bf16[512,2,128]{2,1,0:T(2,128)(2,1)}, u32[]{:S(2)}) copy-start(bf16[512,2,128]{2,1,0:T(2,128)(2,1)} %param.10) | copy-start | bytes 786436
  10.2 9.1 %copy-start.3 = (bf16[512,2,128]{2,1,0:T(2,128)(2,1)S(1)}, bf16[512,2,128]{2,1,0:T(2,128)(2,1)}, u32[]{:S(2)}) copy-start(bf16[512,2,128]{2,1,0:T(2,128)(2,1)} %param.9) | copy-start | bytes 786436
  10.2 107.9 %all-to-all-start = ((bf16[32,512,168]{1,2,0:T(8,128)(2,1)}), bf16[32,512,168]{1,2,0:T(8,128)(2,1)}, u32[]{:S(2)}, u32[]{:S(2)}) async-start(bf16[32,512,168]{1,2,0:T(8,128)(2,1)} %stack.11), calls=%async_computation | async-start | bytes 11010048 | tf_op jit(solution)/shard_map/all_to_all | solution.py:16
  18.0 174.9 %reduce-scatter.2.cloned.1.call-start = ((), (), s32[]{:S(2)}) async-start(), calls=%async_computation.3 | async-start | bytes 6193152 | tf_op jit(solution)/shard_map/reduce_scatter | solution.py:84
  19.4 3.4 %copy-start = (bf16[512,4,128]{2,1,0:T(4,128)(2,1)S(1)}, bf16[512,4,128]{2,1,0:T(4,128)(2,1)}, u32[]{:S(2)}) copy-start(bf16[512,4,128]{2,1,0:T(4,128)(2,1)} %param.8) | copy-start | bytes 1572868
  19.9 2.9 %copy-start.1 = (bf16[1,512,2,128]{3,1,2,0:T(8,128)(2,1)}, bf16[1,512,2,128]{3,1,2,0:T(8,128)(2,1)S(1)}, u32[]{:S(2)}) copy-start(bf16[1,512,2,128]{3,1,2,0:T(8,128)(2,1)S(1)} %fusion.24) | copy-start | bytes 786436
  20.7 70.3 %collective-permute-start = (bf16[2,512,2,128]{3,1,2,0:T(8,128)(2,1)}, bf16[2,512,2,128]{3,1,2,0:T(8,128)(2,1)}, u32[]{:S(2)}, u32[]{:S(2)}) collective-permute-start(bf16[2,512,2,128]{3,1,2,0:T(8,128)(2,1)} %pad_maximum_fusion), channel_id=1, source_target_pairs={{0,8},{8,16},{16,24},{24,32},{32,40},{40,48},{48,56},{56,64},{64,7... | collective-permute-start | bytes 1572872 | tf_op jit(solution)/shard_map/ppermute | solution.py:22
  23.1 80.7 %copy-start.2 = (bf16[1,512,2,128]{3,1,2,0:T(8,128)(2,1)S(1)}, bf16[1,512,2,128]{3,1,2,0:T(8,128)(2,1)}, u32[]{:S(2)}) copy-start(bf16[1,512,2,128]{3,1,2,0:T(8,128)(2,1)} %copy-done.1) | copy-start | bytes 786436
  25.3 79.7 %copy-start.5 = (bf16[512,4,128]{2,1,0:T(4,128)(2,1)S(1)}, bf16[512,4,128]{2,1,0:T(4,128)(2,1)}, u32[]{:S(2)}) copy-start(bf16[512,4,128]{2,1,0:T(4,128)(2,1)} %fusion.16) | copy-start | bytes 1572868
  91.0 12.8 %collective-permute-start.1 = (bf16[2,512,2,128]{3,1,2,0:T(8,128)(2,1)}, bf16[2,512,2,128]{3,1,2,0:T(8,128)(2,1)S(1)}, u32[]{:S(2)}, u32[]{:S(2)}) collective-permute-start(bf16[2,512,2,128]{3,1,2,0:T(8,128)(2,1)} %collective-permute-done), channel_id=1, source_target_pairs={{0,8},{8,16},{16,24},{24,32},{32,40},{40,48},{48,56},{56,64},{64,7... | collective-permute-start | bytes 1572872 | tf_op jit(solution)/shard_map/ppermute | solution.py:22
  125.5 80.7 %copy-start.4 = (bf16[512,672]{0,1:T(8,128)(2,1)S(1)}, bf16[512,672]{0,1:T(8,128)(2,1)}, u32[]{:S(2)}) copy-start(bf16[512,672]{0,1:T(8,128)(2,1)} %param.13) | copy-start | bytes 2064388
  125.5 80.7 %copy-start.7 = (f32[672]{0:T(1024)S(1)}, f32[672]{0:T(1024)}, u32[]{:S(2)}) copy-start(f32[672]{0:T(1024)} %param.12) | copy-start | bytes 8068
Sparse Core Ops, SparseCore 0:
  125.6 67.2 reduce-scatter.1
